TPU v7x, 32 devices: a whole 2x2x4 slice. The times are simulated.
32 devices in a mesh: visit: 8 (over z, core), grp: 4 (over y, x).
Axes of the slice: x: 2, y: 2, z: 4, core: 2. Of those that a mesh axis runs over, the one named last changes fastest.
Arguments:
- coadd_tiles: float32 [2048, 8192], P('visit', 'grp'), may hold values from -9 to 9
- science: float32 [2048, 8192], P('visit', 'grp'), may hold values from -16 to 16
- correlation: int32 [8], P('visit'), may hold values from 0 to 7, as said below
- offset: int32 [8], P('visit'), may hold values from 10 to 246
Outputs:
- difference: float32 [2048, 8192], P('visit', 'grp')
- significance: float32 [2048, 8192], P('visit', 'grp')
- match_coef: float32 [8, 6], P('visit')
Inputs may be any that keep to these rules, and one draw needn't show every extreme that they name: correlation is a permutation of 0 .. 7.
All inputs are finite; a program needn't handle non-finite values.
Results may differ from a plain program's by a relative error of at most 0.0003.
Values sent between devices are 32-bit elements; how exact they have to be, the bound alone decides.
A program may use at most 128 MiB of HBM per device.

v0:
```python
import jax
import jax.numpy as jnp
from jax import lax
from jax.sharding import PartitionSpec as P

ROWS = 256
COLS = 2048
KER_HALF = 10
BASIS = 5
FILT_HALF = 6


ridge = 0.05
epsilon = 1e-06


def extended(x, sides, width):
    for axis, dim in sides:
        size, length = (lax.axis_size(axis), x.shape[dim])
        up = [(i, (i + 1) % size) for i in range(size - 1)]
        down = [(j, i) for i, j in up]
        last = lax.slice_in_dim(x, length - width, length, axis=dim)
        initial = lax.slice_in_dim(x, 0, width, axis=dim)
        before = lax.ppermute(last, axis, up)
        after = lax.ppermute(initial, axis, down)
        x = jnp.concatenate([before, x, after], axis=dim)
    return x


def gauss_taps(spread, half_width):
    points = jnp.arange(-half_width, half_width + 1).astype(jnp.float32)
    return jnp.exp(-points * points / (2.0 * spread * spread))


def basis_taps():
    points = jnp.arange(-KER_HALF, KER_HALF + 1).astype(jnp.float32)
    narrow = gauss_taps(1.0, KER_HALF)
    middle = gauss_taps(1.8, KER_HALF)
    wide_gauss = gauss_taps(3.2, KER_HALF)
    slope_taps = points * middle / 1.8
    row_taps = jnp.stack([narrow, middle, wide_gauss, slope_taps, middle])
    col_taps = jnp.stack([narrow, middle, wide_gauss, middle, slope_taps])
    scales = jnp.sqrt(jnp.sum(row_taps * row_taps, 1) * jnp.sum(col_taps * col_taps, 1))
    return (row_taps / scales[:, None], col_taps)


def filter_taps():
    smooth = gauss_taps(2.0, FILT_HALF)
    return smooth / jnp.sqrt(jnp.sum(smooth * smooth))


def taps_matrix(kernel_taps, step_len):
    half_width = (kernel_taps.shape[1] - 1) // 2
    input_pos = jnp.arange(step_len + 2 * half_width)[:, None]
    output_pos = jnp.arange(step_len)[None, :]
    distance = input_pos - output_pos
    inside = (distance >= 0) & (distance <= 2 * half_width)
    picked = kernel_taps[:, jnp.clip(distance, 0, 2 * half_width)]
    return jnp.where(inside[None], picked, 0.0)


def block_anchors(extent, step_len):
    anchors = list(range(0, extent - step_len + 1, step_len))
    leftover = extent - (anchors[-1] + step_len)
    return (anchors, leftover)


def joined(result, axis_pos):
    layout = result.shape
    merged = layout[:axis_pos] + (-1,) + layout[axis_pos + 2 :]
    return result.reshape(merged)


def along_cols(image_in, kernel_taps):
    half_width = (kernel_taps.shape[1] - 1) // 2
    extent = image_in.shape[1] - 2 * half_width
    step_len = min(256, extent)
    anchors, leftover = block_anchors(extent, step_len)
    windows = jnp.stack(
        [image_in[:, anchor : anchor + step_len + 2 * half_width] for anchor in anchors], 1
    )
    result = jnp.einsum(
        "hnk,ckm->chnm",
        windows,
        taps_matrix(kernel_taps, step_len),
        precision=lax.Precision.HIGHEST,
    )
    return joined(result, 2)


def along_rows(layers, kernel_taps):
    half_width = (kernel_taps.shape[1] - 1) // 2
    extent = layers.shape[1] - 2 * half_width
    step_len = min(256, extent)
    anchors, leftover = block_anchors(extent, step_len)
    windows = jnp.stack([layers for anchor in anchors], 1)
    result = jnp.einsum(
        "cnkw,ckm->cnmw",
        windows,
        taps_matrix(kernel_taps, step_len),
        precision=lax.Precision.HIGHEST,
    )
    return joined(result, 1)


def build_normal(gram_matrix, basis_sums, counted):
    upper_rows = jnp.concatenate([gram_matrix, basis_sums[:, None]], 1)
    lower_row = jnp.concatenate([basis_sums, jnp.array([counted], jnp.float32)])[None]
    return jnp.concatenate([upper_rows, lower_row], 0) / counted + ridge * jnp.eye(
        BASIS + 1, dtype=jnp.float32
    )


def shards(coadd_tiles, science, correlation, offset):
    row_taps, col_taps = basis_taps()
    smooth = filter_taps()[None]
    visits = lax.axis_size("visit")
    groups = lax.axis_size("grp")
    shift_rows = offset[0]
    span_rows = ROWS + 2 * KER_HALF
    piece_rows = ROWS // visits
    held_pieces = lax.all_to_all(
        coadd_tiles.reshape(visits, piece_rows, COLS),
        "visit",
        split_axis=0,
        concat_axis=0,
        tiled=True,
    )
    all_ids = lax.all_gather(correlation, "visit", axis=0, tiled=True)
    holders = jnp.arange(visits)[None, :]
    first_pick = (all_ids[:, None] == holders).astype(jnp.float32)
    second_pick = (((all_ids + 1) % visits)[:, None] == holders).astype(jnp.float32)
    selector = jnp.stack([first_pick, second_pick], 0)
    outgoing = jnp.einsum("tvh,hrc->tvrc", selector, held_pieces, precision=lax.Precision.HIGHEST)
    arrived = lax.all_to_all(outgoing, "visit", split_axis=1, concat_axis=1, tiled=True)
    window = lax.dynamic_slice_in_dim(
        arrived.reshape(2 * ROWS, COLS), shift_rows - KER_HALF, span_rows, 0
    )
    margin = KER_HALF
    framed = extended(window, (("grp", 1),), margin)
    matched = along_rows(along_cols(framed, col_taps), row_taps)
    basis_flat = matched.reshape(BASIS, -1)
    gram_matrix = jnp.dot(basis_flat, basis_flat.T, precision=lax.Precision.HIGHEST)
    basis_sums = jnp.sum(basis_flat, 1)
    projection = jnp.dot(basis_flat, science.reshape(-1), precision=lax.Precision.HIGHEST)
    science_total = jnp.sum(science)
    gram_matrix, basis_sums, projection, science_total = lax.psum(
        (gram_matrix, basis_sums, projection, science_total), "grp"
    )
    counted = float(ROWS * COLS * groups)
    normal = build_normal(gram_matrix, basis_sums, counted)
    rhs_vector = jnp.concatenate([projection, science_total[None]]) / counted
    factor = jnp.linalg.cholesky(normal)
    halfway = lax.linalg.triangular_solve(factor, rhs_vector[:, None], left_side=True, lower=True)
    coefficients = lax.linalg.triangular_solve(
        factor, halfway, left_side=True, lower=True, transpose_a=True
    )[:, 0]
    difference = (
        science - jnp.sum(coefficients[:BASIS, None, None] * matched, 0) - coefficients[BASIS]
    )
    spread_diff = extended(difference, (("grp", 1),), FILT_HALF)
    row_framed = jnp.pad(spread_diff, ((FILT_HALF, FILT_HALF), (0, 0)))
    filtered = along_rows(along_cols(row_framed, smooth), smooth)[0]
    noise_power = jnp.mean(difference * difference)
    significance = filtered / jnp.sqrt(noise_power + epsilon)
    return (difference, significance, coefficients[None])


def solution(mesh):
    in_specs = (P("visit", "grp"), P("visit", "grp"), P("visit"), P("visit"))
    out_specs = (P("visit", "grp"), P("visit", "grp"), P("visit", None))
    return jax.shard_map(shards, mesh=mesh, in_specs=in_specs, out_specs=out_specs, check_vma=False)
```

profile of v0, /device:TPU:4, one launch (start us, length us, event | category | flops | bytes accessed | tf_op | source)
XLA Modules:
  0.0 796.4 jit_solution(13534501325479163338)
XLA Ops:
  0.6 4.9 all-to-all-start
  7.5 47.2 %all-reduce.1 = s32[8]{0:T(128)S(1)} all-reduce(s32[8]{0:T(128)S(1)} %dynamic-update-slice.3), channel_id=1, replica_groups=mesh['visit'=8,'grp'=4] {'visit'}, use_global_device_ids=true, to_apply=%add.1 | all-reduce | flops 8 | bytes 64
  54.8 2.7 fusion.5
  57.6 4.4 copy.57
  62.0 4.6 all-to-all-start.1
  67.5 232.4 %gather_fusion.1 = f32[70656,5]{1,0:T(8,128)} fusion(f32[5,21]{0,1:T(8,128)S(1)} %copy.54, s32[70656]{0:T(1024)S(1)} %broadcast_clamp_fusion), kind=kCustom, calls=%fused_computation.1 | custom fusion | bytes 3108864 | tf_op jit(solution)/shard_map/gather | solution.py:58
  299.9 20.3 %copy.55 = f32[276,256,5]{1,0,2:T(8,128)} copy(f32[276,256,5]{2,1,0:T(8,128)} %bitcast.247) | data formatting | bytes 2826240 | tf_op jit(solution)/shard_map/gather | solution.py:58
  320.6 232.4 %gather_fusion = f32[70656,5]{1,0:T(8,128)} fusion(f32[5,21]{0,1:T(8,128)S(1)} %copy.52, s32[70656]{0:T(1024)S(1)} %broadcast_clamp_fusion), kind=kCustom, calls=%fused_computation | custom fusion | bytes 3108864 | tf_op jit(solution)/shard_map/gather | solution.py:58
  553.0 20.4 %copy.53 = f32[276,256,5]{1,0,2:T(8,128)} copy(f32[276,256,5]{2,1,0:T(8,128)} %bitcast.246) | data formatting | bytes 2826240 | tf_op jit(solution)/shard_map/gather | solution.py:58
  574.9 1.1 reduce_sum.66
  576.7 2.5 copy.58
  579.3 3.4 collective-permute-start
  583.0 3.6 collective-permute-start.1
  586.5 2.2 collective-permute-done
  590.9 21.1 %convolution_bitcast_fusion = f32[5,276,8,256]{3,1,2,0:T(8,128)S(1)} fusion(f32[276,8,276]{2,0,1:T(8,128)S(1)} %fusion.27, f32[276,256,5]{1,0,2:T(8,128)S(1)} %copy-done.5, pred[276,256]{1,0:T(8,128)(4,1)S(1)} %copy-done.6), kind=kOutput, calls=%fused_computation.7 | convolution fusion | flops 9360860160 | bytes 15226368 | tf_op jit(solution)/shard_map/hnk,ckm->chnm/dot_general | solution.py:82
  611.9 7.8 copy.59
  619.7 10.9 %reshape.328 = f32[5,276,2048]{2,1,0:T(8,128)} reshape(f32[5,276,8,256]{3,2,1,0:T(8,128)} %copy.59) | data formatting | bytes 22609920 | tf_op jit(solution)/shard_map/reshape.14
  630.7 20.5 %fusion.156 = (f32[5]{0:T(128)S(1)}, f32[5,256,2048]{2,1,0:T(8,128)S(1)}) fusion(f32[5,276,2048]{2,1,0:T(8,128)} %reshape.328, f32[276,256,5]{1,0,2:T(8,128)S(1)} %copy-done.4, pred[276,256]{1,0:T(8,128)(4,1)S(1)} %copy-done.7), kind=kOutput, calls=%fused_computation.206 | convolution fusion | flops 8685184000 | bytes 23274516 | tf_op jit(solution)/shard_map/cnkw,ckm->cnmw/dot_general | solution.py:97
  651.1 36.2 %fusion.14 = f32[5,5]{0,1:T(8,128)S(1)} fusion(f32[5,256,2048]{2,1,0:T(8,128)S(1)} %get-tuple-element.27), kind=kOutput, calls=%fused_computation.31 | convolution fusion | flops 157286400 | bytes 10485860 | tf_op jit(solution)/shard_map/dot_general | solution.py:143
  687.4 44.0 %fusion.17 = f32[5]{0:T(128)S(1)} fusion(f32[256,2048,1]{1,0,2:T(8,128)S(1)} %bitcast.256, f32[5,256,2048]{2,1,0:T(8,128)} %copy-done), kind=kOutput, calls=%fused_computation.32 | convolution fusion | flops 31457280 | bytes 12582932 | tf_op jit(solution)/shard_map/dot_general | solution.py:145
  731.3 10.6 %all-reduce.2 = (f32[5]{0:T(128)S(1)}, f32[5,5]{0,1:T(8,128)S(1)}, f32[1]{0:T(128)}, f32[5]{0:T(128)S(1)}) all-reduce(f32[5]{0:T(128)S(1)} %get-tuple-element.26, f32[5,5]{0,1:T(8,128)S(1)} %fusion.14, f32[1]{0:T(128)} %bitcast.32, f32[5]{0:T(128)S(1)} %fusion.17), channel_id=1, replica_groups=mesh['visit'=8,'grp'=4] {'grp'}, use_global_device_ids=true, to_apply=%region_4.5 | all-reduce | flops 36 | bytes 288 | tf_op jit(solution)/shard_map/psum | solution.py:147
  746.5 5.6 multiply_reduce_fusion
  752.1 1.9 multiply_reduce_fusion.1
  754.0 1.3 copy-done.3
  755.5 1.9 collective-permute-start.2
  757.4 4.8 collective-permute-start.3
  763.7 1.0 collective-permute-done.3
  764.7 3.2 concatenate.29
  768.3 12.2 %convolution_bitcast_fusion.1 = f32[1,268,8,256]{3,1,2,0:T(8,128)S(1)} fusion(f32[268,8,268]{2,0,1:T(8,128)S(1)} %fusion.51, f32[]{:T(128)} %bitcast.50, f32[]{:T(128)} %bitcast.51, f32[]{:T(128)} %bitcast.52, f32[]{:T(128)} %bitcast.53, f32[]{:T(128)} %bitcast.54, f32[]{:T(128)} %bitcast.56, f32[]{:T(128)} %bitcast.55, f32[]{:T(128)} %bitcast.39, ...), kind=kOutput, calls=%fused_computation.25 | convolution fusion | flops 1767479296 | bytes 4493876 | tf_op jit(solution)/shard_map/hnk,ckm->chnm/dot_general | solution.py:82
  780.5 1.3 copy.93
  781.9 0.9 copy.75
  782.9 13.0 %convolution_divide_fusion = f32[256,2048]{1,0:T(8,128)} fusion(f32[268,2048]{1,0:T(8,128)S(1)} %bitcast.259, f32[]{:T(128)S(6)} %sqrt.15, f32[]{:T(128)} %bitcast.50, f32[]{:T(128)} %bitcast.51, f32[]{:T(128)} %bitcast.52, f32[]{:T(128)} %bitcast.53, f32[]{:T(128)} %bitcast.54, f32[]{:T(128)} %bitcast.56, f32[]{:T(128)} %bitcast.55, f32[]{:T(128)} %bitcast.39, ...), kind=kOutput, calls=%fused_computation.9 | convolution fusion | flops 1688967168 | bytes 4292664 | tf_op jit(solution)/shard_map/cnkw,ckm->cnmw/dot_general | solution.py:97
  (80 shorter events, 11.9 us)
Async XLA Ops:
  0.6 5.6 copy-start.9
  0.6 54.2 %all-to-all-start = ((f32[8,32,2048]{2,1,0:T(8,128)}), f32[8,32,2048]{2,1,0:T(8,128)S(1)}, u32[]{:S(2)}, u32[]{:S(2)}) async-start(f32[8,32,2048]{2,1,0:T(8,128)} %bitcast.260), calls=%async_computation | async-start | bytes 4194304 | tf_op jit(solution)/shard_map/all_to_all | solution.py:122
  62.0 514.7 %all-to-all-start.1 = ((f32[2,8,32,2048]{3,2,0,1:T(8,128)}), f32[2,8,32,2048]{3,2,0,1:T(8,128)}, u32[]{:S(2)}, u32[]{:S(2)}) async-start(f32[2,8,32,2048]{3,2,0,1:T(8,128)} %copy.57), calls=%async_computation.1 | async-start | bytes 8388608 | tf_op jit(solution)/shard_map/all_to_all | solution.py:135
  553.0 21.9 %copy-start.1 = (f32[256,2048]{1,0:T(8,128)S(1)}, f32[256,2048]{1,0:T(8,128)}, u32[]{:S(2)}) copy-start(f32[256,2048]{1,0:T(8,128)} %param.6) | copy-start | bytes 6291460
  579.3 9.4 %collective-permute-start = (f32[276,10]{1,0:T(8,128)S(1)}, f32[276,10]{1,0:T(8,128)S(1)}, u32[]{:S(2)}, u32[]{:S(2)}) collective-permute-start(f32[276,10]{1,0:T(8,128)S(1)} %get-tuple-element.10), channel_id=1, source_target_pairs={{0,1},{1,2},{2,3},{4,5},{5,6},{6,7},{8,9},{9,10},{10,11},{12,13},{... | collective-permute-start | bytes 33128 | tf_op jit(solution)/shard_map/ppermute | solution.py:24
  583.0 7.7 collective-permute-start.1
  589.3 1.6 copy-start.5
  589.3 1.6 copy-start.6
  619.7 10.9 %copy-start.4 = (f32[276,256,5]{1,0,2:T(8,128)S(1)}, f32[276,256,5]{1,0,2:T(8,128)}, u32[]{:S(2)}) copy-start(f32[276,256,5]{1,0,2:T(8,128)} %copy.53) | copy-start | bytes 4239364
  619.7 10.9 %copy-start.7 = (pred[276,256]{1,0:T(8,128)(4,1)S(1)}, pred[276,256]{1,0:T(8,128)(4,1)}, u32[]{:S(2)}) copy-start(pred[276,256]{1,0:T(8,128)(4,1)} %fusion.54) | copy-start | bytes 211972
  651.1 36.2 %copy-start = (f32[5,256,2048]{2,1,0:T(8,128)}, f32[5,256,2048]{2,1,0:T(8,128)S(1)}, u32[]{:S(2)}) copy-start(f32[5,256,2048]{2,1,0:T(8,128)S(1)} %get-tuple-element.27) | copy-start | bytes 31457284
  651.1 36.2 %copy-start.2 = (f32[256,2048]{1,0:T(8,128)S(1)}, f32[256,2048]{1,0:T(8,128)}, u32[]{:S(2)}) copy-start(f32[256,2048]{1,0:T(8,128)} %param.6) | copy-start | bytes 6291460
  745.9 6.2 copy-start.8
  754.0 1.3 copy-start.3
  755.5 8.2 %collective-permute-start.2 = (f32[256,6]{1,0:T(8,128)S(1)}, f32[256,6]{1,0:T(8,128)S(1)}, u32[]{:S(2)}, u32[]{:S(2)}) collective-permute-start(f32[256,6]{1,0:T(8,128)S(1)} %get-tuple-element.12), channel_id=1, source_target_pairs={{0,1},{1,2},{2,3},{4,5},{5,6},{6,7},{8,9},{9,10},{10,11},{12,13},{... | collective-permute-start | bytes 18440 | tf_op jit(solution)/shard_map/ppermute | solution.py:24
  757.4 7.3 collective-permute-start.3
where the time goes:
time: 806 us; the launch traced here: 796 us
  local copies, waits for them, and re-layouts  543 us (67%)
  matrix products  151 us (19%)
  blocking collectives  57.8 us (7%)
  starting transfers between devices  23.1 us (3%)
  other arithmetic  13.6 us (2%)
    gather x5, local copies, waits for them, and re-layouts, taps_matrix(): picked = kernel_taps[:, jnp.clip(distance, 0, 2 * half_width)]  506 us
    unnamed x1, blocking collectives  47.2 us
    dot_general x1, matrix products, shards(): jnp.dot(basis_flat, science.reshape(-1), precision=lax.Precision.HIGHEST)  44 us
    dot_general x1, matrix products, shards(): jnp.dot(basis_flat, basis_flat.T, precision=lax.Precision.HIGHEST)  36.2 us
    dot_general x2, matrix products, along_rows(): jnp.einsum('cnkw,ckm->cnmw', windows, taps_matrix(kernel_taps, step_len),...  33.5 us
    dot_general x2, matrix products, along_cols(): jnp.einsum('hnk,ckm->chnm', windows, taps_matrix(kernel_taps, step_len),...  33.3 us
  transfers between devices with their start and end apart: 6, of which 3 were waited for; matrix products, arithmetic and copies ran while one was open for 64% of the time, Pallas kernels for 0%

commit v1 on v0

--- a/solution.py
+++ b/solution.py
@@ -54,9 +54,10 @@
     input_pos = jnp.arange(step_len + 2 * half_width)[:, None]
     output_pos = jnp.arange(step_len)[None, :]
     distance = input_pos - output_pos
-    inside = (distance >= 0) & (distance <= 2 * half_width)
-    picked = kernel_taps[:, jnp.clip(distance, 0, 2 * half_width)]
-    return jnp.where(inside[None], picked, 0.0)
+    result = jnp.zeros((kernel_taps.shape[0],) + distance.shape, jnp.float32)
+    for tap in range(2 * half_width + 1):
+        result = jnp.where((distance == tap)[None], kernel_taps[:, tap][:, None, None], result)
+    return result
 
 
 def block_anchors(extent, step_len):
@@ -116,26 +117,21 @@
     smooth = filter_taps()[None]
     visits = lax.axis_size("visit")
     groups = lax.axis_size("grp")
-    shift_rows = offset[0]
     span_rows = ROWS + 2 * KER_HALF
-    piece_rows = ROWS // visits
-    held_pieces = lax.all_to_all(
-        coadd_tiles.reshape(visits, piece_rows, COLS),
-        "visit",
-        split_axis=0,
-        concat_axis=0,
-        tiled=True,
+    tile_rows, tile_cols = coadd_tiles.shape
+    strip = lax.all_to_all(coadd_tiles, "visit", split_axis=1, concat_axis=0, tiled=True)
+    places = lax.all_gather(
+        correlation * tile_rows + offset - KER_HALF, "visit", axis=0, tiled=True
     )
-    all_ids = lax.all_gather(correlation, "visit", axis=0, tiled=True)
-    holders = jnp.arange(visits)[None, :]
-    first_pick = (all_ids[:, None] == holders).astype(jnp.float32)
-    second_pick = (((all_ids + 1) % visits)[:, None] == holders).astype(jnp.float32)
-    selector = jnp.stack([first_pick, second_pick], 0)
-    outgoing = jnp.einsum("tvh,hrc->tvrc", selector, held_pieces, precision=lax.Precision.HIGHEST)
-    arrived = lax.all_to_all(outgoing, "visit", split_axis=1, concat_axis=1, tiled=True)
-    window = lax.dynamic_slice_in_dim(
-        arrived.reshape(2 * ROWS, COLS), shift_rows - KER_HALF, span_rows, 0
+    strip = jnp.concatenate([strip, strip[:span_rows]], 0)
+    outgoing = jnp.stack(
+        [
+            lax.dynamic_slice_in_dim(strip, places[v] % (visits * tile_rows), span_rows, 0)
+            for v in range(visits)
+        ],
+        0,
     )
+    window = lax.all_to_all(outgoing, "visit", split_axis=0, concat_axis=2, tiled=True)[0]
     margin = KER_HALF
     framed = extended(window, (("grp", 1),), margin)
     matched = along_rows(along_cols(framed, col_taps), row_taps)

time: 806 us -> 378 us (0.47)
  local copies, waits for them, and re-layouts: 543 us -> 42.2 us
  waiting for transfers between devices: 3.76 us -> 41.8 us
  other arithmetic: 13.6 us -> 38.7 us
  between operations: 4.23 us -> 20.3 us
    gather x5 -> x0, local copies, waits for them, and re-layouts: 506 us -> none  [taps_matrix(): picked = kernel_taps[:, jnp.clip(distance, 0, 2 * half_width)]]
    all_to_all x2, waiting for transfers between devices: 0.01 us -> 40 us  [the longest x1 40 us: shards(): lax.all_to_all(outgoing, 'visit', split_axis=0, concat_axis=2, tiled=True)]
    select_n x2 -> x1, other arithmetic: 0.06 us -> 9.08 us  [taps_matrix(): jnp.where((distance == tap)[None], kernel_taps[:, tap][:, None, None], re...]
  transfers between devices with their start and end apart: 6 -> 6, of which waited for: 3 -> 2; matrix products, arithmetic and copies ran while one was open for 64% -> 8% of each run, Pallas kernels for 0% -> 0%
where the time goes in v1:
time: 378 us; the launch traced here: 372 us
  matrix products  149 us (39%)
  blocking collectives  57.2 us (15%)
  local copies, waits for them, and re-layouts  42.2 us (11%)
  waiting for transfers between devices  41.8 us (11%)
  other arithmetic  38.7 us (10%)
  starting transfers between devices  22.4 us (6%)
  between operations  20.3 us (5%)
    unnamed x1, blocking collectives  46.6 us
    dot_general x1, matrix products, shards(): jnp.dot(basis_flat, science.reshape(-1), precision=lax.Precision.HIGHEST)  43.8 us
    all_to_all x1, waiting for transfers between devices, shards(): lax.all_to_all(outgoing, 'visit', split_axis=0, concat_axis=2, tiled=True)  40 us
    dot_general x2, matrix products, along_cols(): jnp.einsum('hnk,ckm->chnm', windows, taps_matrix(kernel_taps, step_len),...  37.1 us
    dot_general x1, matrix products, shards(): jnp.dot(basis_flat, basis_flat.T, precision=lax.Precision.HIGHEST)  36.6 us
    dot_general x2, matrix products, along_rows(): jnp.einsum('cnkw,ckm->cnmw', windows, taps_matrix(kernel_taps, step_len),...  31 us
    another operation x1, local copies, waits for them, and re-layouts  11.1 us
    psum x1, blocking collectives, shards(): lax.psum((gram_matrix, basis_sums, projection, science_total), 'grp')  10.6 us
  transfers between devices with their start and end apart: 6, of which 2 were waited for; matrix products, arithmetic and copies ran while one was open for 8% of the time, Pallas kernels for 0%

profile of v1, /device:TPU:4, one launch (start us, length us, event | category | flops | bytes accessed | tf_op | source)
XLA Modules:
  0.0 372.0 jit_solution(14254142472250550608)
XLA Ops:
  0.6 2.9 copy.55
  3.5 5.0 %all-to-all-start = ((f32[256,8,256]{0,2,1:T(8,128)}), f32[256,8,256]{0,2,1:T(8,128)S(1)}, u32[]{:S(2)}, u32[]{:S(2)}) async-start(f32[256,8,256]{0,2,1:T(8,128)} %bitcast.217), calls=%async_computation | async-start | bytes 4194304 | tf_op jit(solution)/shard_map/all_to_all | solution.py:122
  11.2 46.6 %all-reduce.1 = s32[8]{0:T(128)S(1)} all-reduce(s32[8]{0:T(128)S(1)} %add_dynamic-update-slice_fusion), channel_id=1, replica_groups=mesh['visit'=8,'grp'=4] {'visit'}, use_global_device_ids=true, to_apply=%add.1 | all-reduce | flops 8 | bytes 64
  73.7 1.3 copy-done.3
  75.0 1.9 copy.56
  83.8 3.6 all-to-all-start.1
  90.5 1.1 slice_reduce_fusion.20
  91.7 1.1 slice_reduce_fusion.41
  100.6 40.0 %all-to-all-done.1 = f32[8,276,256]{2,1,0:T(8,128)S(1)} async-done(((f32[8,276,256]{2,1,0:T(8,128)}), f32[8,276,256]{2,1,0:T(8,128)S(1)}, u32[]{:S(2)}, u32[]{:S(2)}) %all-to-all-start.1) | async-done | bytes 2261024 | tf_op jit(solution)/shard_map/all_to_all | solution.py:134
  141.4 1.0 copy.74
  142.5 3.4 collective-permute-start
  146.7 2.8 reduce_sum.66
  149.5 3.5 collective-permute-start.1
  154.7 1.8 collective-permute-done.1
  157.1 24.9 %convolution_bitcast_fusion = f32[5,276,8,256]{3,1,2,0:T(8,128)S(1)} fusion(f32[276,8,276]{2,0,1:T(8,128)S(1)} %fusion.145, f32[5]{0:T(128)S(1)} %copy-done.62, f32[5]{0:T(128)S(1)} %copy-done.63, f32[5]{0:T(128)S(1)} %copy-done.64, f32[5]{0:T(128)S(1)} %copy-done.65, f32[5]{0:T(128)S(1)} %copy-done.66, f32[5]{0:T(128)S(1)} %copy-done.67, ...), kind=kOutput, calls=%fused_computation.13 | convolution fusion | flops 9367925760 | bytes 15226788 | tf_op jit(solution)/shard_map/hnk,ckm->chnm/dot_general | solution.py:83
  182.0 7.8 %copy.58 = f32[5,276,8,256]{3,2,1,0:T(8,128)} copy(f32[5,276,8,256]{3,1,2,0:T(8,128)S(1)} %convolution_bitcast_fusion) | data formatting | bytes 22609920 | tf_op jit(solution)/shard_map/hnk,ckm->chnm/transpose | solution.py:83
  190.2 11.1 %reshape.548 = f32[5,276,2048]{2,1,0:T(8,128)} reshape(f32[5,276,8,256]{3,2,1,0:T(8,128)} %copy.58) | data formatting | bytes 22609920 | tf_op jit(solution)/shard_map/reshape.13
  201.6 26.1 %fusion.323 = (f32[5]{0:T(128)S(1)}, f32[5,256,2048]{2,1,0:T(8,128)S(1)}) fusion(f32[5,276,2048]{2,1,0:T(8,128)} %reshape.548, f32[5]{0:T(128)S(1)} %get-tuple-element.4, f32[5]{0:T(128)S(1)} %get-tuple-element.5, f32[5]{0:T(128)S(1)} %get-tuple-element.6, f32[5]{0:T(128)S(1)} %get-tuple-element.7, f32[5]{0:T(128)S(1)} %copy-done.47, f32[5]{0:T(128)S(1)} %copy-done.48, ...), kind=kOutput, calls=%fused_computation.423 | convolution fusion | flops 8692249600 | bytes 23274936 | tf_op jit(solution)/shard_map/cnkw,ckm->cnmw/dot_general | solution.py:98
  227.7 36.6 %fusion.50 = f32[5,5]{0,1:T(8,128)S(1)} fusion(f32[5,256,2048]{2,1,0:T(8,128)S(1)} %get-tuple-element.77), kind=kOutput, calls=%fused_computation.82 | convolution fusion | flops 157286400 | bytes 10485860 | tf_op jit(solution)/shard_map/dot_general | solution.py:139
  264.3 43.8 %fusion.53 = f32[5]{0:T(128)S(1)} fusion(f32[256,2048,1]{1,0,2:T(8,128)S(1)} %bitcast.210, f32[5,256,2048]{2,1,0:T(8,128)} %copy-done), kind=kOutput, calls=%fused_computation.83 | convolution fusion | flops 31457280 | bytes 12582932 | tf_op jit(solution)/shard_map/dot_general | solution.py:141
  308.1 10.6 %all-reduce.2 = (f32[5]{0:T(128)S(1)}, f32[5,5]{0,1:T(8,128)S(1)}, f32[1]{0:T(128)}, f32[5]{0:T(128)S(1)}) all-reduce(f32[5]{0:T(128)S(1)} %get-tuple-element.76, f32[5,5]{0,1:T(8,128)S(1)} %fusion.50, f32[1]{0:T(128)} %bitcast.42, f32[5]{0:T(128)S(1)} %fusion.53), channel_id=1, replica_groups=mesh['visit'=8,'grp'=4] {'grp'}, use_global_device_ids=true, to_apply=%region_4.5 | all-reduce | flops 36 | bytes 288 | tf_op jit(solution)/shard_map/psum | solution.py:143
  323.3 5.6 %multiply_reduce_fusion = f32[256,2048]{1,0:T(8,128)S(1)} fusion(f32[5,256,2048]{2,1,0:T(8,128)} %copy-done, f32[5]{0:T(128)S(1)} %bitcast.221), kind=kLoop, calls=%fused_computation.4 | loop fusion | flops 4718592 | bytes 12582932 | tf_op jit(solution)/shard_map/reduce_sum | solution.py:155
  328.9 1.9 multiply_reduce_fusion.1
  330.8 1.3 copy-done.2
  332.2 1.9 collective-permute-start.2
  334.2 5.0 %collective-permute-start.3 = (f32[256,6]{1,0:T(8,128)S(1)}, f32[256,6]{1,0:T(8,128)S(1)}, u32[]{:S(2)}, u32[]{:S(2)}) collective-permute-start(f32[256,6]{1,0:T(8,128)S(1)} %get-tuple-element.53), channel_id=1, source_target_pairs={{1,0},{2,1},{3,2},{5,4},{6,5},{7,6},{9,8},{10,9},{11,10},{13,12},{... | collective-permute-start | bytes 18440 | tf_op jit(solution)/shard_map/ppermute | solution.py:25
  339.2 9.1 %compare_select_fusion.12 = f32[1,268,1,256]{3,2,1,0:T(1,128)S(1)} fusion(f32[]{:T(128)} %bitcast.60, f32[]{:T(128)} %bitcast.59, f32[]{:T(128)} %bitcast.58, f32[]{:T(128)} %bitcast.57, f32[]{:T(128)} %bitcast.56, f32[]{:T(128)} %bitcast.55, f32[]{:T(128)} %bitcast.54, f32[]{:T(128)} %bitcast.53, f32[]{:T(128)} %bitcast.52, f32[]{:T(128)} %bitcast.51, ...), kind=kLoop, calls=%fused_computation.97 | loop fusion | flops 1852416 | bytes 274484 | tf_op jit(solution)/shard_map/jit(_where)/select_n | solution.py:59
  349.0 3.0 concatenate.33
  352.3 12.2 %convolution_bitcast_fusion.1 = f32[1,268,8,256]{3,1,2,0:T(8,128)S(1)} fusion(f32[268,8,268]{2,0,1:T(8,128)S(1)} %fusion.169, f32[]{:T(128)} %bitcast.60, f32[]{:T(128)} %bitcast.59, f32[]{:T(128)} %bitcast.58, f32[]{:T(128)} %bitcast.57, f32[]{:T(128)} %bitcast.56, f32[]{:T(128)} %bitcast.55, f32[]{:T(128)} %bitcast.54, f32[]{:T(128)} %bitcast.53, ...), kind=kOutput, calls=%fused_computation.37 | convolution fusion | flops 1766999040 | bytes 4493876 | tf_op jit(solution)/shard_map/hnk,ckm->chnm/dot_general | solution.py:83
  364.5 1.3 copy.95
  366.0 0.9 copy.75
  366.9 4.9 %convolution_divide_fusion = f32[256,2048]{1,0:T(8,128)} fusion(f32[268,2048]{1,0:T(8,128)S(1)} %bitcast.218, f32[]{:T(128)S(6)} %sqrt.15, f32[1,268,1,256]{3,2,1,0:T(1,128)S(1)} %compare_select_fusion.12), kind=kOutput, calls=%fused_computation.15 | convolution fusion | flops 1686634496 | bytes 4567044 | tf_op jit(solution)/shard_map/cnkw,ckm->cnmw/dot_general | solution.py:98
  (241 shorter events, 27.8 us)
Async XLA Ops:
  3.5 70.1 %all-to-all-start = ((f32[256,8,256]{0,2,1:T(8,128)}), f32[256,8,256]{0,2,1:T(8,128)S(1)}, u32[]{:S(2)}, u32[]{:S(2)}) async-start(f32[256,8,256]{0,2,1:T(8,128)} %bitcast.217), calls=%async_computation | async-start | bytes 4194304 | tf_op jit(solution)/shard_map/all_to_all | solution.py:122
  83.8 56.8 %all-to-all-start.1 = ((f32[8,276,256]{2,1,0:T(8,128)}), f32[8,276,256]{2,1,0:T(8,128)S(1)}, u32[]{:S(2)}, u32[]{:S(2)}) async-start(f32[8,276,256]{2,1,0:T(8,128)} %fusion.172), calls=%async_computation.1 | async-start | bytes 4587520 | tf_op jit(solution)/shard_map/all_to_all | solution.py:134
  142.5 10.5 %collective-permute-start = (f32[276,10]{1,0:T(8,128)S(1)}, f32[276,10]{1,0:T(8,128)S(1)}, u32[]{:S(2)}, u32[]{:S(2)}) collective-permute-start(f32[276,10]{1,0:T(8,128)S(1)} %get-tuple-element.52), channel_id=1, source_target_pairs={{0,1},{1,2},{2,3},{4,5},{5,6},{6,7},{8,9},{9,10},{10,11},{12,13},{... | collective-permute-start | bytes 33128 | tf_op jit(solution)/shard_map/ppermute | solution.py:24
  149.5 7.0 %collective-permute-start.1 = (f32[276,10]{1,0:T(8,128)S(1)}, f32[276,10]{1,0:T(8,128)S(1)}, u32[]{:S(2)}, u32[]{:S(2)}) collective-permute-start(f32[276,10]{1,0:T(8,128)S(1)} %get-tuple-element.51), channel_id=1, source_target_pairs={{1,0},{2,1},{3,2},{5,4},{6,5},{7,6},{9,8},{10,9},{11,10},{13,12},{... | collective-permute-start | bytes 33128 | tf_op jit(solution)/shard_map/ppermute | solution.py:25
  189.8 11.4 %copy-start.13 = (pred[276,256]{1,0:T(8,128)(4,1)S(1)}, pred[276,256]{1,0:T(8,128)(4,1)}, u32[]{:S(2)}) copy-start(pred[276,256]{1,0:T(8,128)(4,1)} %get-tuple-element.83) | copy-start | bytes 211972
  189.9 11.4 %copy-start.15 = (pred[276,256]{1,0:T(8,128)(4,1)S(1)}, pred[276,256]{1,0:T(8,128)(4,1)}, u32[]{:S(2)}) copy-start(pred[276,256]{1,0:T(8,128)(4,1)} %get-tuple-element.84) | copy-start | bytes 211972
  189.9 11.4 %copy-start.17 = (pred[276,256]{1,0:T(8,128)(4,1)S(1)}, pred[276,256]{1,0:T(8,128)(4,1)}, u32[]{:S(2)}) copy-start(pred[276,256]{1,0:T(8,128)(4,1)} %get-tuple-element.85) | copy-start | bytes 211972
  189.9 11.4 %copy-start.19 = (pred[276,256]{1,0:T(8,128)(4,1)S(1)}, pred[276,256]{1,0:T(8,128)(4,1)}, u32[]{:S(2)}) copy-start(pred[276,256]{1,0:T(8,128)(4,1)} %get-tuple-element.86) | copy-start | bytes 211972
  189.9 11.4 %copy-start.21 = (pred[276,256]{1,0:T(8,128)(4,1)S(1)}, pred[276,256]{1,0:T(8,128)(4,1)}, u32[]{:S(2)}) copy-start(pred[276,256]{1,0:T(8,128)(4,1)} %get-tuple-element.87) | copy-start | bytes 211972
  189.9 11.4 %copy-start.23 = (pred[276,256]{1,0:T(8,128)(4,1)S(1)}, pred[276,256]{1,0:T(8,128)(4,1)}, u32[]{:S(2)}) copy-start(pred[276,256]{1,0:T(8,128)(4,1)} %get-tuple-element.88) | copy-start | bytes 211972
  189.9 11.4 %copy-start.25 = (pred[276,256]{1,0:T(8,128)(4,1)S(1)}, pred[276,256]{1,0:T(8,128)(4,1)}, u32[]{:S(2)}) copy-start(pred[276,256]{1,0:T(8,128)(4,1)} %get-tuple-element.89) | copy-start | bytes 211972
  189.9 11.4 %copy-start.27 = (pred[276,256]{1,0:T(8,128)(4,1)S(1)}, pred[276,256]{1,0:T(8,128)(4,1)}, u32[]{:S(2)}) copy-start(pred[276,256]{1,0:T(8,128)(4,1)} %get-tuple-element.90) | copy-start | bytes 211972
  189.9 11.4 %copy-start.29 = (pred[276,256]{1,0:T(8,128)(4,1)S(1)}, pred[276,256]{1,0:T(8,128)(4,1)}, u32[]{:S(2)}) copy-start(pred[276,256]{1,0:T(8,128)(4,1)} %get-tuple-element.91) | copy-start | bytes 211972
  189.9 11.4 %copy-start.31 = (pred[276,256]{1,0:T(8,128)(4,1)S(1)}, pred[276,256]{1,0:T(8,128)(4,1)}, u32[]{:S(2)}) copy-start(pred[276,256]{1,0:T(8,128)(4,1)} %get-tuple-element.92) | copy-start | bytes 211972
  189.9 11.4 %copy-start.33 = (pred[276,256]{1,0:T(8,128)(4,1)S(1)}, pred[276,256]{1,0:T(8,128)(4,1)}, u32[]{:S(2)}) copy-start(pred[276,256]{1,0:T(8,128)(4,1)} %get-tuple-element.93) | copy-start | bytes 211972
  190.0 11.4 %copy-start.35 = (pred[276,256]{1,0:T(8,128)(4,1)S(1)}, pred[276,256]{1,0:T(8,128)(4,1)}, u32[]{:S(2)}) copy-start(pred[276,256]{1,0:T(8,128)(4,1)} %get-tuple-element.94) | copy-start | bytes 211972
  190.0 11.4 %copy-start.37 = (pred[276,256]{1,0:T(8,128)(4,1)S(1)}, pred[276,256]{1,0:T(8,128)(4,1)}, u32[]{:S(2)}) copy-start(pred[276,256]{1,0:T(8,128)(4,1)} %get-tuple-element.95) | copy-start | bytes 211972
  190.0 11.4 %copy-start.39 = (pred[276,256]{1,0:T(8,128)(4,1)S(1)}, pred[276,256]{1,0:T(8,128)(4,1)}, u32[]{:S(2)}) copy-start(pred[276,256]{1,0:T(8,128)(4,1)} %get-tuple-element.96) | copy-start | bytes 211972
  190.0 11.4 %copy-start.41 = (pred[276,256]{1,0:T(8,128)(4,1)S(1)}, pred[276,256]{1,0:T(8,128)(4,1)}, u32[]{:S(2)}) copy-start(pred[276,256]{1,0:T(8,128)(4,1)} %get-tuple-element.97) | copy-start | bytes 211972
  190.0 11.4 %copy-start.43 = (pred[276,256]{1,0:T(8,128)(4,1)S(1)}, pred[276,256]{1,0:T(8,128)(4,1)}, u32[]{:S(2)}) copy-start(pred[276,256]{1,0:T(8,128)(4,1)} %get-tuple-element.98) | copy-start | bytes 211972
  190.0 11.4 %copy-start.45 = (pred[276,256]{1,0:T(8,128)(4,1)S(1)}, pred[276,256]{1,0:T(8,128)(4,1)}, u32[]{:S(2)}) copy-start(pred[276,256]{1,0:T(8,128)(4,1)} %get-tuple-element.99) | copy-start | bytes 211972
  190.0 11.4 %copy-start.47 = (f32[5]{0:T(128)S(1)}, f32[5]{0:T(128)}, u32[]{:S(2)}) copy-start(f32[5]{0:T(128)} %get-tuple-element.8) | copy-start | bytes 64
  190.0 11.4 %copy-start.48 = (f32[5]{0:T(128)S(1)}, f32[5]{0:T(128)}, u32[]{:S(2)}) copy-start(f32[5]{0:T(128)} %get-tuple-element.9) | copy-start | bytes 64
  190.0 11.4 %copy-start.49 = (f32[5]{0:T(128)S(1)}, f32[5]{0:T(128)}, u32[]{:S(2)}) copy-start(f32[5]{0:T(128)} %get-tuple-element.10) | copy-start | bytes 64
  190.0 11.4 %copy-start.50 = (f32[5]{0:T(128)S(1)}, f32[5]{0:T(128)}, u32[]{:S(2)}) copy-start(f32[5]{0:T(128)} %get-tuple-element.11) | copy-start | bytes 64
  190.1 11.4 %copy-start.51 = (f32[5]{0:T(128)S(1)}, f32[5]{0:T(128)}, u32[]{:S(2)}) copy-start(f32[5]{0:T(128)} %get-tuple-element.12) | copy-start | bytes 64
  190.1 11.4 %copy-start.52 = (f32[5]{0:T(128)S(1)}, f32[5]{0:T(128)}, u32[]{:S(2)}) copy-start(f32[5]{0:T(128)} %get-tuple-element.13) | copy-start | bytes 64
  190.1 11.4 %copy-start.53 = (f32[5]{0:T(128)S(1)}, f32[5]{0:T(128)}, u32[]{:S(2)}) copy-start(f32[5]{0:T(128)} %get-tuple-element.14) | copy-start | bytes 64
  227.7 36.6 %copy-start = (f32[5,256,2048]{2,1,0:T(8,128)}, f32[5,256,2048]{2,1,0:T(8,128)S(1)}, u32[]{:S(2)}) copy-start(f32[5,256,2048]{2,1,0:T(8,128)S(1)} %get-tuple-element.77) | copy-start | bytes 31457284
  227.7 36.6 %copy-start.1 = (f32[256,2048]{1,0:T(8,128)S(1)}, f32[256,2048]{1,0:T(8,128)}, u32[]{:S(2)}) copy-start(f32[256,2048]{1,0:T(8,128)} %param.6) | copy-start | bytes 6291460
  332.2 16.8 %collective-permute-start.2 = (f32[256,6]{1,0:T(8,128)S(1)}, f32[256,6]{1,0:T(8,128)S(1)}, u32[]{:S(2)}, u32[]{:S(2)}) collective-permute-start(f32[256,6]{1,0:T(8,128)S(1)} %get-tuple-element.54), channel_id=1, source_target_pairs={{0,1},{1,2},{2,3},{4,5},{5,6},{6,7},{8,9},{9,10},{10,11},{12,13},{... | collective-permute-start | bytes 18440 | tf_op jit(solution)/shard_map/ppermute | solution.py:24
  334.2 14.8 %collective-permute-start.3 = (f32[256,6]{1,0:T(8,128)S(1)}, f32[256,6]{1,0:T(8,128)S(1)}, u32[]{:S(2)}, u32[]{:S(2)}) collective-permute-start(f32[256,6]{1,0:T(8,128)S(1)} %get-tuple-element.53), channel_id=1, source_target_pairs={{1,0},{2,1},{3,2},{5,4},{6,5},{7,6},{9,8},{10,9},{11,10},{13,12},{... | collective-permute-start | bytes 18440 | tf_op jit(solution)/shard_map/ppermute | solution.py:25
  (57 other events, 274.0 us)
